TPU v7x, 256 devices: a whole 4x4x8 slice. The times are simulated.
256 devices in a mesh: seq: 32 (over z_lo, x, core), tp: 8 (over y, z_hi).
Axes of the slice: x: 4, y: 4, z: 8 (z_hi: 2, z_lo: 4; z = z_hi * 4 + z_lo), core: 2. Of those that a mesh axis runs over, the one named last changes fastest.
Arguments:
- hidden: bfloat16 [8192, 7168], P('seq', 'tp'), may hold values from -6 to 6
- norm_gain: bfloat16 [7168], replicated, may hold values from 0.5 to 1.5
- w_query: bfloat16 [7168, 4096], P(None, 'tp'), may hold values from -0.0625 to 0.0625
- w_key: bfloat16 [7168, 1024], P(None, 'tp'), may hold values from -0.0625 to 0.0625
- w_value: bfloat16 [7168, 1024], P(None, 'tp'), may hold values from -0.0625 to 0.0625
- prefix_keys: bfloat16 [8192, 1024], P('seq', 'tp'), may hold values from -64 to 64
- prefix_values: bfloat16 [8192, 1024], P('seq', 'tp'), may hold values from -6 to 6
- page_prefix: int32 [64], replicated, may hold values from 0 to 3, as said below
- request_prefix: int32 [32], replicated, may hold values from 0 to 3
- suffix_lengths: int32 [32], replicated, may hold values from 1 to 1024, 8192 in all
- row_order: int32 [8192], replicated, may hold values from 0 to 8191, as said below
Outputs:
- attended: bfloat16 [8192, 4096], P('seq', 'tp')
- suffix_keys: bfloat16 [8192, 1024], P('seq', 'tp')
- suffix_values: bfloat16 [8192, 1024], P('seq', 'tp')
Inputs may be any that keep to these rules, and one draw needn't show every extreme that they name: `page_prefix`: each of the 4 prefixes owns exactly 16 pages. `suffix_lengths`: the lengths sum to 8192; the longest is exactly 1024. `row_order`: a permutation of 0 to 8191 made of aligned runs of 128 consecutive values.
All inputs are finite; a program needn't handle non-finite values.
Results may differ from a plain program's by a relative error of at most 0.0075.
The roundings to bfloat16 on the way count: a program that leaves them out, or rounds other values in their place, can miss the bound.
Values may be sent and summed in bfloat16 or wider, within the bound.
A program may use at most 128 MiB of HBM per device.

v0:
```python
import math
import jax
import jax.numpy as jnp
from jax import lax
from jax.sharding import PartitionSpec as P

HEAD = 128
PAGE = 128
PREFIXES = 4
ROPE_BASE = 5000000.0


def rotate(tensor_in, positions):
    head_dim = tensor_in.shape[-1]
    half_dim = head_dim // 2
    frequency = ROPE_BASE ** (-(jnp.arange(half_dim, dtype=jnp.float32) * 2.0 / head_dim))
    angles = positions.astype(jnp.float32)[:, None] * frequency[None, :]
    cosine = jnp.cos(angles)[:, None, :]
    sine_part = jnp.sin(angles)[:, None, :]
    first_half = tensor_in[..., :half_dim]
    second_half = tensor_in[..., half_dim:]
    return jnp.concatenate(
        [
            first_half * cosine - second_half * sine_part,
            second_half * cosine + first_half * sine_part,
        ],
        axis=-1,
    )


def locate(row_order, suffix_lengths, request_prefix):
    end_rows = jnp.cumsum(suffix_lengths)
    starts = end_rows - suffix_lengths
    numbers = jnp.arange(suffix_lengths.shape[0], dtype=jnp.int32)
    request = jnp.sum((row_order[:, None] >= end_rows[None, :]).astype(jnp.int32), axis=1)
    chosen = request[:, None] == numbers[None, :]
    position = row_order - jnp.sum(jnp.where(chosen, starts[None, :], 0), axis=1)
    wanted = jnp.sum(jnp.where(chosen, request_prefix[None, :], 0), axis=1)
    return (request, position, wanted)


def body(
    hidden,
    norm_gain,
    w_query,
    w_key,
    w_value,
    prefix_keys,
    prefix_values,
    page_prefix,
    request_prefix,
    suffix_lengths,
    row_order,
):
    gathered = lax.all_gather(hidden, "tp", axis=1, tiled=True)
    local_rows = gathered.shape[0]
    hidden_f = gathered.astype(jnp.float32)
    mean_sq = jnp.mean(hidden_f * hidden_f, axis=1, keepdims=True)
    normed = (
        hidden_f * lax.rsqrt(mean_sq + 1e-05) * norm_gain.astype(jnp.float32)[None, :]
    ).astype(jnp.bfloat16)
    request_all, position_all, wanted_all = locate(row_order, suffix_lengths, request_prefix)
    offset = lax.axis_index("seq") * local_rows
    request = lax.dynamic_slice_in_dim(request_all, offset, local_rows)
    position = lax.dynamic_slice_in_dim(position_all, offset, local_rows)
    wanted = lax.dynamic_slice_in_dim(wanted_all, offset, local_rows)
    prefix_len = page_prefix.shape[0] * PAGE // PREFIXES
    rope_at = prefix_len + position
    q_heads = w_query.shape[1] // HEAD
    kv_heads = w_key.shape[1] // HEAD
    group_size = q_heads // kv_heads
    queries = rotate(
        jnp.dot(normed, w_query, preferred_element_type=jnp.float32).reshape(
            local_rows, q_heads, HEAD
        ),
        rope_at,
    ).astype(jnp.bfloat16)
    queries = queries.reshape(local_rows, kv_heads, group_size, HEAD)
    new_keys = rotate(
        jnp.dot(normed, w_key, preferred_element_type=jnp.float32).reshape(
            local_rows, kv_heads, HEAD
        ),
        rope_at,
    ).astype(jnp.bfloat16)
    new_keys = new_keys.reshape(local_rows, kv_heads * HEAD)
    new_values = jnp.dot(normed, w_value, preferred_element_type=jnp.float32).astype(jnp.bfloat16)
    row_pages = jnp.repeat(page_prefix, PAGE)
    score_scale = 1.0 / math.sqrt(HEAD)
    initial = (
        jnp.full((kv_heads, local_rows, group_size), -1e30, jnp.float32),
        jnp.zeros((kv_heads, local_rows, group_size), jnp.float32),
        jnp.zeros((kv_heads, local_rows, group_size, HEAD), jnp.float32),
    )

    def attend(state, key_rows, value_rows, visible):
        row_count = key_rows.shape[0]
        block_width = math.gcd(row_count, 512)
        block_count = row_count // block_width
        key_blocks = key_rows.reshape(block_count, block_width, kv_heads, HEAD)
        value_blocks = value_rows.reshape(block_count, block_width, kv_heads, HEAD)
        mask_blocks = visible.reshape(local_rows, block_count, block_width).transpose(1, 0, 2)

        def step(carry_in, inputs):
            run_max, run_sum, run_acc = carry_in
            key_block, value_block, mask_block = inputs
            scores = (
                jnp.einsum("tngd,knd->ntgk", queries, key_block, preferred_element_type=jnp.float32)
                * score_scale
            )
            seen = mask_block[None, :, None, :]
            new_max = jnp.maximum(run_max, jnp.max(jnp.where(seen, scores, -1e30), axis=-1))
            weights = jnp.where(seen, jnp.exp(scores - new_max[..., None]), 0.0)
            fade = jnp.exp(run_max - new_max)
            run_sum = run_sum * fade + jnp.sum(weights, axis=-1)
            run_acc = run_acc * fade[..., None] + jnp.einsum(
                "ntgk,knd->ntgd",
                weights.astype(jnp.bfloat16),
                value_block,
                preferred_element_type=jnp.float32,
            )
            return ((new_max, run_sum, run_acc), None)

        result, unused = lax.scan(step, state, (key_blocks, value_blocks, mask_blocks))
        return result

    key_rows = lax.all_gather(prefix_keys, "seq", axis=0, tiled=True)
    value_rows = lax.all_gather(prefix_values, "seq", axis=0, tiled=True)
    visible = wanted[:, None] == row_pages[None, :]
    state = attend(initial, key_rows, value_rows, visible)
    key_rows = lax.all_gather(new_keys, "seq", axis=0, tiled=True)
    value_rows = lax.all_gather(new_values, "seq", axis=0, tiled=True)
    visible = (request[:, None] == request_all[None, :]) & (
        position_all[None, :] <= position[:, None]
    )
    state = attend(state, key_rows, value_rows, visible)
    run_max, run_sum, run_acc = state
    attended = (
        (run_acc / run_sum[..., None])
        .transpose(1, 0, 2, 3)
        .reshape(local_rows, q_heads * HEAD)
        .astype(jnp.bfloat16)
    )
    return (attended, new_keys, new_values)


def solution(mesh):
    return jax.shard_map(
        body,
        mesh=mesh,
        in_specs=(
            P("seq", "tp"),
            P(),
            P(None, "tp"),
            P(None, "tp"),
            P(None, "tp"),
            P("seq", "tp"),
            P("seq", "tp"),
            P(),
            P(),
            P(),
            P(),
        ),
        out_specs=(P("seq", "tp"), P("seq", "tp"), P("seq", "tp")),
        check_vma=False,
    )
```

profile of v0, /device:TPU:1, one launch (start us, length us, event | category | flops | bytes accessed | tf_op | source)
XLA Modules:
  0.0 437.9 jit_solution(14165126439068676029)
XLA Ops:
  14.6 98.3 %all-gather.8.cloned.1.call-done = bf16[256,7168]{1,0:T(8,128)(2,1)} async-done(((bf16[256,896]{1,0:T(8,128)(2,1)}), bf16[256,7168]{1,0:T(8,128)(2,1)}) %all-gather.8.cloned.1.call-update) | async-done | bytes 3670032 | tf_op jit(solution)/shard_map/all_gather | solution.py:55
  112.9 3.0 fusion.44
  116.0 1.5 convolution_bitcast_fusion.2
  119.7 2.8 broadcast_compare_fusion
  122.5 4.7 %compare_and_fusion = pred[16,256,512]{1,2,0:T(8,128)(4,1)} fusion(s32[256]{0:T(256)S(1)} %get-tuple-element.194, s32[16,512]{1,0:T(8,128)S(1)} %le.17, s32[16,512]{1,0:T(8,128)S(1)} %eq.52, s32[256]{0:T(256)S(1)} %dynamic_slice.31), kind=kLoop, calls=%fused_computation.60 | loop fusion | flops 6291456 | bytes 2164736 | tf_op jit(solution)/shard_map/and | solution.py:132
  127.2 6.0 %fusion.61 = f32[256,512]{1,0:T(8,128)} fusion(bf16[7168,512]{1,0:T(8,128)(2,1)} %param.17, bf16[256,7168]{1,0:T(8,128)(2,1)S(1)} %copy-done.3, f32[7168]{0:T(1024)S(1)} %convert_element_type.47, f32[256]{0:T(256)S(1)} %add_rsqrt_fusion), kind=kOutput, calls=%fused_computation.97 | convolution fusion | flops 1886388224 | bytes 11564032 | tf_op jit(solution)/shard_map/dot_general | solution.py:73
  135.0 1.4 copy-done.4
  136.5 3.5 convolution_convert_fusion
  140.0 30.5 %all-gather.6.cloned.1.call-done = bf16[8192,128]{1,0:T(8,128)(2,1)} async-done(((bf16[256,128]{1,0:T(8,128)(2,1)}), bf16[8192,128]{1,0:T(8,128)(2,1)}) %all-gather.6.cloned.1.call-update) | async-done | bytes 2097168 | tf_op jit(solution)/shard_map/all_gather | solution.py:126
  170.4 60.9 %all-gather.10.cloned.1.call-done = bf16[8192,128]{1,0:T(8,128)(2,1)} async-done(((bf16[256,128]{1,0:T(8,128)(2,1)}), bf16[8192,128]{1,0:T(8,128)(2,1)}) %all-gather.10.cloned.1.call-update) | async-done | bytes 2097168 | tf_op jit(solution)/shard_map/all_gather | solution.py:127
  231.4 107.4 %while.30 = (s32[]{:T(128)}, f32[1,256,4]{1,2,0:T(4,128)S(1)}, f32[1,256,4]{1,2,0:T(4,128)S(1)}, f32[1,256,4,128]{3,1,2,0:T(8,128)S(1)}, pred[16,256,512]{1,2,0:...) while((s32[]{:T(128)}, f32[1,256,4]{1,2,0:T(4,128)S(1)}, ...), condition=%wide.region_8.9_spmd.clone, body=%wide.region_5.8_spmd.clone.sunk | while | flops 274601984 | bytes 16974992 | solution.py:123
  232.3 2.7 fusion.87
  235.0 2.5 fusion.90
  239.0 2.7 fusion.87
  241.7 2.5 fusion.90
  245.7 2.7 fusion.87
  248.4 2.5 fusion.90
  252.4 2.7 fusion.87
  255.1 2.5 fusion.90
  259.1 2.7 fusion.87
  261.9 2.5 fusion.90
  265.8 2.7 fusion.87
  268.6 2.6 fusion.90
  272.6 2.7 fusion.87
  275.3 2.6 fusion.90
  279.3 2.7 fusion.87
  282.0 2.6 fusion.90
  286.0 2.7 fusion.87
  288.7 2.5 fusion.90
  292.7 2.7 fusion.87
  295.4 2.5 fusion.90
  299.4 2.7 fusion.87
  302.1 2.5 fusion.90
  306.1 2.7 fusion.87
  308.8 2.5 fusion.90
  312.8 2.7 fusion.87
  315.5 2.5 fusion.90
  319.5 2.7 fusion.87
  322.2 2.6 fusion.90
  326.3 2.7 fusion.87
  329.0 2.6 fusion.90
  333.0 2.7 fusion.87
  335.7 2.5 fusion.90
  339.5 4.1 copy.43
  343.6 14.1 %all-gather.14.cloned.1.call-done = bf16[8192,128]{1,0:T(8,128)(2,1)} async-done(((bf16[256,128]{1,0:T(8,128)(2,1)}), bf16[8192,128]{1,0:T(8,128)(2,1)}) %all-gather.14.cloned.1.call-update) | async-done | bytes 2097168 | tf_op jit(solution)/shard_map/all_gather | solution.py:131
  357.6 72.6 %while.29 = (s32[]{:T(128)}, f32[1,256,4]{1,2,0:T(4,128)S(1)}, f32[1,256,4]{1,2,0:T(4,128)S(1)}, f32[1,256,4,128]{3,1,2,0:T(8,128)S(1)}, pred[16,256,512]{1,2,0:...) while((s32[]{:T(128)}, f32[1,256,4]{1,2,0:T(4,128)S(1)}, ...), condition=%wide.region_12.13_spmd, body=%wide.region_9.12_spmd.sunk | while | flops 274467840 | bytes 8586337 | solution.py:123
  360.0 1.7 fusion.84
  364.5 1.7 fusion.84
  369.0 1.7 fusion.84
  372.2 1.4 fusion.81
  373.6 1.7 fusion.84
  376.7 1.4 fusion.81
  378.1 1.7 fusion.84
  382.6 1.7 fusion.84
  387.2 1.7 fusion.84
  391.7 1.7 fusion.84
  396.3 1.7 fusion.84
  400.8 1.7 fusion.84
  405.3 1.7 fusion.84
  409.9 1.7 fusion.84
  414.4 1.7 fusion.84
  419.0 1.7 fusion.84
  423.5 1.7 fusion.84
  428.0 1.7 fusion.84
  (260 shorter events, 78.0 us)
Async XLA Ops:
  7.2 108.7 %copy-start = (bf16[7168,128]{1,0:T(8,128)(2,1)S(1)}, bf16[7168,128]{1,0:T(8,128)(2,1)}, u32[]{:S(2)}) copy-start(bf16[7168,128]{1,0:T(8,128)(2,1)} %param.18) | copy-start | bytes 5505028
  7.2 105.7 %all-gather.8.cloned.1.call-start = ((), (), s32[]{:S(2)}) async-start(), calls=%async_computation.1 | async-start | bytes 4128768 | tf_op jit(solution)/shard_map/all_gather | solution.py:55
  7.9 162.5 %all-gather.6.cloned.1.call-start = ((), (), s32[]{:S(2)}) async-start(), calls=%async_computation | async-start | bytes 2162688 | tf_op jit(solution)/shard_map/all_gather | solution.py:126
  8.7 222.7 %all-gather.10.cloned.1.call-start = ((), (), s32[]{:S(2)}) async-start(), calls=%async_computation.2 | async-start | bytes 2162688 | tf_op jit(solution)/shard_map/all_gather | solution.py:127
  9.4 330.1 %all-gather.12.cloned.1.call-start = ((), (), s32[]{:S(2)}) async-start(), calls=%async_computation.3 | async-start | bytes 2162688 | tf_op jit(solution)/shard_map/all_gather | solution.py:130
  112.9 3.1 copy-start.2
  116.0 3.0 copy-start.6
  118.6 239.1 %all-gather.14.cloned.1.call-start = ((), (), s32[]{:S(2)}) async-start(), calls=%async_computation.4 | async-start | bytes 2162688 | tf_op jit(solution)/shard_map/all_gather | solution.py:131
  119.7 7.5 %copy-start.3 = (bf16[256,7168]{1,0:T(8,128)(2,1)S(1)}, bf16[256,7168]{1,0:T(8,128)(2,1)}, u32[]{:S(2)}) copy-start(bf16[256,7168]{1,0:T(8,128)(2,1)} %all-gather.8.cloned.1.call-done) | copy-start | bytes 11010052
  134.4 2.1 copy-start.4
  231.4 107.4 %copy-start.5 = (bf16[256,128]{0,1:T(8,128)(2,1)S(1)}, bf16[256,128]{0,1:T(8,128)(2,1)}, u32[]{:S(2)}) copy-start(bf16[256,128]{0,1:T(8,128)(2,1)} %pad_maximum_fusion.1) | copy-start | bytes 196612
  235.0 2.6 copy-start.1
  241.7 2.6 copy-start.1
  248.4 2.6 copy-start.1
  255.1 2.6 copy-start.1
  261.8 2.6 copy-start.1
  268.5 2.6 copy-start.1
  275.3 2.6 copy-start.1
  282.0 2.6 copy-start.1
  288.7 2.6 copy-start.1
  295.4 2.6 copy-start.1
  302.1 2.6 copy-start.1
  308.8 2.6 copy-start.1
  315.5 2.6 copy-start.1
  322.2 2.6 copy-start.1
  329.0 2.6 copy-start.1
  335.7 2.6 copy-start.1
Sparse Core Ops, SparseCore 0:
  10.6 102.2 all-gather.7
  114.7 55.6 all-gather.5
  172.3 59.0 all-gather.9
  233.6 62.8 all-gather.11
  298.7 58.8 all-gather.13
where the time goes:
time: 440 us; the launch traced here: 438 us
  waiting for transfers between devices  206 us (47%)
  matrix products  144 us (33%)
  local copies, waits for them, and re-layouts  39.5 us (9%)
  other arithmetic  32.5 us (7%)
  between operations  13.9 us (3%)
    all_gather x1, waiting for transfers between devices, body(): gathered = lax.all_gather(hidden, 'tp', axis=1, tiled=True)  98.3 us
    dot_general x32, matrix products, step(): jnp.einsum('ntgk,knd->ntgd', weights.astype(jnp.bfloat16), value_block, p...  67.7 us
    dot_general x32, matrix products, step(): jnp.einsum('tngd,knd->ntgk', queries, key_block, preferred_element_type=j...  65.6 us
    all_gather x1, waiting for transfers between devices, body(): value_rows = lax.all_gather(prefix_values, 'seq', axis=0, tiled=True)  60.9 us
    all_gather x1, waiting for transfers between devices, body(): key_rows = lax.all_gather(prefix_keys, 'seq', axis=0, tiled=True)  30.5 us
    broadcast_in_dim x32, local copies, waits for them, and re-layouts, step(): jnp.where(seen, scores, -1e+30)  29.4 us
    reduce_sum x32, other arithmetic, step(): run_sum = run_sum * fade + jnp.sum(weights, axis=-1)  14.8 us
    all_gather x1, waiting for transfers between devices, body(): value_rows = lax.all_gather(new_values, 'seq', axis=0, tiled=True)  14.1 us
  transfers between devices with their start and end apart: 5, of which 4 were waited for; matrix products, arithmetic and copies ran while one was open for 32% of the time, Pallas kernels for 0%

commit v1 on v0

--- a/solution.py
+++ b/solution.py
@@ -124,7 +124,9 @@
         return result
 
     key_rows = lax.all_gather(prefix_keys, "seq", axis=0, tiled=True)
-    value_rows = lax.all_gather(prefix_values, "seq", axis=0, tiled=True)
+    value_rows = jnp.concatenate(
+        lax.all_to_all(jnp.stack(lax.axis_size("seq") * [prefix_values]), "seq", 0, 0), axis=0
+    )
     visible = wanted[:, None] == row_pages[None, :]
     state = attend(initial, key_rows, value_rows, visible)
     key_rows = lax.all_gather(new_keys, "seq", axis=0, tiled=True)

time: 440 us -> 393 us (0.89)
  waiting for transfers between devices: 206 us -> 152 us
  starting transfers between devices: 0.37 us -> 6.05 us
    all_gather x1 -> x0, waiting for transfers between devices: 60.9 us -> none  [body(): value_rows = lax.all_gather(prefix_values, 'seq', axis=0, tiled=True)]
    all_to_all x0 -> x1, waiting for transfers between devices: none -> 36.5 us  [body(): lax.all_to_all(jnp.stack(lax.axis_size('seq') * [prefix_values]), 'seq',...]
    all_gather x1, waiting for transfers between devices: 30.5 us -> 2.14 us  [body(): key_rows = lax.all_gather(prefix_keys, 'seq', axis=0, tiled=True)]
    all_to_all x0 -> x1, starting transfers between devices: none -> 5.72 us  [body(): lax.all_to_all(jnp.stack(lax.axis_size('seq') * [prefix_values]), 'seq',...]
  transfers between devices with their start and end apart: 5 -> 5, of which waited for: 4 -> 4; matrix products, arithmetic and copies ran while one was open for 32% -> 37% of each run, Pallas kernels for 0% -> 0%
where the time goes in v1:
time: 393 us; the launch traced here: 391 us
  waiting for transfers between devices  152 us (39%)
  matrix products  145 us (37%)
  local copies, waits for them, and re-layouts  39.9 us (10%)
  other arithmetic  32.3 us (8%)
  between operations  13.9 us (4%)
  starting transfers between devices  6.05 us (2%)
    all_gather x1, waiting for transfers between devices, body(): gathered = lax.all_gather(hidden, 'tp', axis=1, tiled=True)  99 us
    dot_general x32, matrix products, step(): jnp.einsum('ntgk,knd->ntgd', weights.astype(jnp.bfloat16), value_block, p...  67.7 us
    dot_general x32, matrix products, step(): jnp.einsum('tngd,knd->ntgk', queries, key_block, preferred_element_type=j...  65.4 us
    all_to_all x1, waiting for transfers between devices, body(): lax.all_to_all(jnp.stack(lax.axis_size('seq') * [prefix_values]), 'seq',...  36.5 us
    broadcast_in_dim x32, local copies, waits for them, and re-layouts, step(): jnp.where(seen, scores, -1e+30)  29.4 us
    reduce_sum x32, other arithmetic, step(): run_sum = run_sum * fade + jnp.sum(weights, axis=-1)  14.8 us
    all_gather x1, waiting for transfers between devices, body(): value_rows = lax.all_gather(new_values, 'seq', axis=0, tiled=True)  13.3 us
  transfers between devices with their start and end apart: 5, of which 4 were waited for; matrix products, arithmetic and copies ran while one was open for 37% of the time, Pallas kernels for 0%

profile of v1, /device:TPU:1, one launch (start us, length us, event | category | flops | bytes accessed | tf_op | source)
XLA Modules:
  0.0 391.3 jit_solution(14127002408386061200)
XLA Ops:
  13.9 99.0 %all-gather.7.cloned.1.call-done = bf16[256,7168]{1,0:T(8,128)(2,1)} async-done(((bf16[256,896]{1,0:T(8,128)(2,1)}), bf16[256,7168]{1,0:T(8,128)(2,1)}) %all-gather.7.cloned.1.call-update) | async-done | bytes 3670032 | tf_op jit(solution)/shard_map/all_gather | solution.py:55
  112.9 3.0 fusion.44
  116.0 1.5 convolution_bitcast_fusion.2
  118.6 1.8 stack.2
  120.4 5.7 %all-to-all-start = ((bf16[32,256,128]{2,1,0:T(8,128)(2,1)}), bf16[32,256,128]{2,1,0:T(8,128)(2,1)}, u32[]{:S(2)}, u32[]{:S(2)}) async-start(bf16[32,256,128]{2,1,0:T(8,128)(2,1)} %stack.2), calls=%async_computation | async-start | bytes 4194304 | tf_op jit(solution)/shard_map/all_to_all | solution.py:128
  127.3 2.7 broadcast_compare_fusion
  129.9 4.6 %compare_and_fusion = pred[16,256,512]{1,2,0:T(8,128)(4,1)} fusion(s32[256]{0:T(256)S(1)} %get-tuple-element.194, s32[16,512]{1,0:T(8,128)S(1)} %le.17, s32[16,512]{1,0:T(8,128)S(1)} %eq.52, s32[256]{0:T(256)S(1)} %dynamic_slice.31), kind=kLoop, calls=%fused_computation.60 | loop fusion | flops 6291456 | bytes 2164736 | tf_op jit(solution)/shard_map/and | solution.py:134
  134.5 6.0 %fusion.61 = f32[256,512]{1,0:T(8,128)} fusion(bf16[7168,512]{1,0:T(8,128)(2,1)} %param.17, bf16[256,7168]{1,0:T(8,128)(2,1)S(1)} %copy-done.3, f32[7168]{0:T(1024)S(1)} %convert_element_type.47, f32[256]{0:T(256)S(1)} %add_rsqrt_fusion), kind=kOutput, calls=%fused_computation.97 | convolution fusion | flops 1886388224 | bytes 11564032 | tf_op jit(solution)/shard_map/dot_general | solution.py:73
  141.8 4.5 %convolution_convert_fusion = bf16[256,128]{1,0:T(8,128)(2,1)} fusion(bf16[7168,128]{1,0:T(8,128)(2,1)} %param.19, bf16[256,7168]{1,0:T(8,128)(2,1)} %all-gather.7.cloned.1.call-done, f32[7168]{0:T(1024)S(1)} %convert_element_type.47, f32[256]{0:T(256)S(1)} %add_rsqrt_fusion), kind=kOutput, calls=%fused_computation.66 | convolution fusion | flops 477134848 | bytes 5600256 | tf_op jit(solution)/shard_map/dot_general | solution.py:86
  147.0 36.5 %all-to-all-done = bf16[32,256,128]{2,1,0:T(8,128)(2,1)} async-done(((bf16[32,256,128]{2,1,0:T(8,128)(2,1)}), bf16[32,256,128]{2,1,0:T(8,128)(2,1)}, u32[]{:S(2)}, u32[]{:S(2)}) %all-to-all-start) | async-done | bytes 2097184 | tf_op jit(solution)/shard_map/all_to_all | solution.py:128
  183.5 2.1 all-gather.5.cloned.1.call-done
  185.7 107.2 %while.30 = (s32[]{:T(128)}, f32[1,256,4]{1,2,0:T(4,128)S(1)}, f32[1,256,4]{1,2,0:T(4,128)S(1)}, f32[1,256,4,128]{3,1,2,0:T(8,128)S(1)}, pred[16,256,512]{1,2,0:...) while((s32[]{:T(128)}, f32[1,256,4]{1,2,0:T(4,128)S(1)}, ...), condition=%wide.region_8.9_spmd.clone, body=%wide.region_5.8_spmd.clone.sunk | while | flops 274601984 | bytes 16974992 | solution.py:123
  186.6 2.7 fusion.87
  189.3 2.5 fusion.90
  193.3 2.7 fusion.87
  196.0 2.6 fusion.90
  200.0 2.7 fusion.87
  202.7 2.5 fusion.90
  206.7 2.7 fusion.87
  209.4 2.5 fusion.90
  213.4 2.7 fusion.87
  216.1 2.5 fusion.90
  220.1 2.7 fusion.87
  222.8 2.5 fusion.90
  226.8 2.7 fusion.87
  229.5 2.5 fusion.90
  233.5 2.7 fusion.87
  236.2 2.5 fusion.90
  240.2 2.7 fusion.87
  242.9 2.5 fusion.90
  246.9 2.7 fusion.87
  249.6 2.5 fusion.90
  253.6 2.7 fusion.87
  256.3 2.5 fusion.90
  260.2 2.7 fusion.87
  263.0 2.5 fusion.90
  266.9 2.7 fusion.87
  269.6 2.6 fusion.90
  273.7 2.7 fusion.87
  276.4 2.5 fusion.90
  280.3 2.7 fusion.87
  283.1 2.6 fusion.90
  287.1 2.7 fusion.87
  289.8 2.6 fusion.90
  293.6 4.1 %copy.43 = bf16[8192,128]{1,0:T(8,128)(2,1)} copy(bf16[8192,128]{0,1:T(8,128)(2,1)} %all-gather.9.cloned.1.call-done) | data formatting | bytes 4194304 | tf_op jit(solution)/shard_map/while | solution.py:123
  297.7 13.3 %all-gather.11.cloned.1.call-done = bf16[8192,128]{1,0:T(8,128)(2,1)} async-done(((bf16[256,128]{1,0:T(8,128)(2,1)}), bf16[8192,128]{1,0:T(8,128)(2,1)}) %all-gather.11.cloned.1.call-update) | async-done | bytes 2097168 | tf_op jit(solution)/shard_map/all_gather | solution.py:133
  311.0 72.6 %while.29 = (s32[]{:T(128)}, f32[1,256,4]{1,2,0:T(4,128)S(1)}, f32[1,256,4]{1,2,0:T(4,128)S(1)}, f32[1,256,4,128]{3,1,2,0:T(8,128)S(1)}, pred[16,256,512]{1,2,0:...) while((s32[]{:T(128)}, f32[1,256,4]{1,2,0:T(4,128)S(1)}, ...), condition=%wide.region_12.13_spmd, body=%wide.region_9.12_spmd.sunk | while | flops 274467840 | bytes 8586337 | solution.py:123
  313.3 1.7 fusion.84
  317.9 1.7 fusion.84
  322.4 1.7 fusion.84
  325.5 1.4 fusion.81
  326.9 1.7 fusion.84
  331.5 1.7 fusion.84
  336.0 1.7 fusion.84
  340.6 1.7 fusion.84
  345.1 1.7 fusion.84
  349.6 1.7 fusion.84
  354.2 1.7 fusion.84
  358.7 1.7 fusion.84
  363.2 1.7 fusion.84
  367.8 1.7 fusion.84
  372.3 1.7 fusion.84
  376.9 1.7 fusion.84
  381.4 1.7 fusion.84
  (260 shorter events, 78.7 us)
Async XLA Ops:
  7.2 108.7 %copy-start = (bf16[7168,128]{1,0:T(8,128)(2,1)S(1)}, bf16[7168,128]{1,0:T(8,128)(2,1)}, u32[]{:S(2)}) copy-start(bf16[7168,128]{1,0:T(8,128)(2,1)} %param.18) | copy-start | bytes 5505028
  7.2 105.7 %all-gather.7.cloned.1.call-start = ((), (), s32[]{:S(2)}) async-start(), calls=%async_computation.2 | async-start | bytes 4128768 | tf_op jit(solution)/shard_map/all_gather | solution.py:55
  7.9 177.7 %all-gather.5.cloned.1.call-start = ((), (), s32[]{:S(2)}) async-start(), calls=%async_computation.1 | async-start | bytes 2162688 | tf_op jit(solution)/shard_map/all_gather | solution.py:126
  8.7 284.9 %all-gather.9.cloned.1.call-start = ((), (), s32[]{:S(2)}) async-start(), calls=%async_computation.3 | async-start | bytes 2162688 | tf_op jit(solution)/shard_map/all_gather | solution.py:132
  112.9 3.1 copy-start.2
  116.0 2.5 copy-start.5
  120.4 6.2 %copy-start.6 = (s32[64]{0:T(128)S(1)}, s32[64]{0:T(128)}, u32[]{:S(2)}) copy-start(s32[64]{0:T(128)} %param.22) | copy-start | bytes 772
  120.4 63.1 %all-to-all-start = ((bf16[32,256,128]{2,1,0:T(8,128)(2,1)}), bf16[32,256,128]{2,1,0:T(8,128)(2,1)}, u32[]{:S(2)}, u32[]{:S(2)}) async-start(bf16[32,256,128]{2,1,0:T(8,128)(2,1)} %stack.2), calls=%async_computation | async-start | bytes 4194304 | tf_op jit(solution)/shard_map/all_to_all | solution.py:128
  126.1 184.9 %all-gather.11.cloned.1.call-start = ((), (), s32[]{:S(2)}) async-start(), calls=%async_computation.4 | async-start | bytes 2162688 | tf_op jit(solution)/shard_map/all_gather | solution.py:133
  127.3 7.3 %copy-start.3 = (bf16[256,7168]{1,0:T(8,128)(2,1)S(1)}, bf16[256,7168]{1,0:T(8,128)(2,1)}, u32[]{:S(2)}) copy-start(bf16[256,7168]{1,0:T(8,128)(2,1)} %all-gather.7.cloned.1.call-done) | copy-start | bytes 11010052
  185.7 107.2 %copy-start.4 = (bf16[256,128]{0,1:T(8,128)(2,1)S(1)}, bf16[256,128]{0,1:T(8,128)(2,1)}, u32[]{:S(2)}) copy-start(bf16[256,128]{0,1:T(8,128)(2,1)} %pad_maximum_fusion.1) | copy-start | bytes 196612
  189.3 2.6 copy-start.1
  196.0 2.6 copy-start.1
  202.7 2.6 copy-start.1
  209.4 2.6 copy-start.1
  216.1 2.6 copy-start.1
  222.8 2.6 copy-start.1
  229.5 2.6 copy-start.1
  236.2 2.6 copy-start.1
  242.9 2.6 copy-start.1
  249.6 2.6 copy-start.1
  256.3 2.6 copy-start.1
  262.9 2.6 copy-start.1
  269.6 2.6 copy-start.1
  276.4 2.6 copy-start.1
  283.0 2.6 copy-start.1
  289.7 2.6 copy-start.1
Sparse Core Ops, SparseCore 0:
  10.6 102.2 all-gather.6
  114.7 70.8 all-gather.4
  188.0 61.7 all-gather.8
  252.1 58.8 all-gather.10
